TPU v7x, 256 devices: a whole 4x4x8 slice. The times are simulated.
256 devices in a mesh: blk: 64 (over z, x, y_hi), aux: 4 (over y_lo, core).
Axes of the slice: x: 4, y: 4 (y_hi: 2, y_lo: 2; y = y_hi * 2 + y_lo), z: 8, core: 2. Of those that a mesh axis runs over, the one named last changes fastest.
Arguments:
- coeffs: bfloat16 [16384, 512], P('blk'), may hold values from -6 to 6
- fitting: bfloat16 [16384, 256, 256], P('blk', 'aux'), may hold values from -0.375 to 0.375
- screen: int32 [256, 4], P('blk'), may hold values from 0 to 255, as said below
- counts: int32 [256], P('blk'), may hold values from 1 to 4, as said below
- tile_order: int32 [64, 16], P('blk'), may hold values from 0 to 15, each once within a row
Outputs:
- fock_tiles: float32 [1024, 4096], P(('blk', 'aux'))
Inputs may be any that keep to these rules, and one draw needn't show every extreme that they name: `screen`: each partner block lies on the same index of blk as its basis block or on one of the two indices before or after it, counted around the axis. `counts`: some block uses all 4 slots and some block only one.
All inputs are finite; a program needn't handle non-finite values.
Results may differ from a plain program's by a relative error of at most 0.0003.
Values may be sent and summed in bfloat16 or wider, within the bound.
A program may use at most 128 MiB of HBM per device.

v0:
```python
import jax
import jax.numpy as jnp
from jax import lax
from jax.sharding import PartitionSpec as P


def passed_along(value, axis, by):
    length = lax.axis_size(axis)
    return lax.ppermute(value, axis, [(i, (i + by) % length) for i in range(length)])


def per_device(coeffs, fitting, screen, counts, tile_order):
    blocks_here = screen.shape[0]
    slot_count = screen.shape[1]
    block_width = coeffs.shape[0] // blocks_here
    orbitals = coeffs.shape[1]
    aux_here = fitting.shape[1]
    loop_size = lax.axis_size("blk")
    position = lax.axis_index("blk")
    earlier = []
    later = []
    moving_up = coeffs
    moving_down = coeffs
    for step in range(2):
        moving_up = passed_along(moving_up, "blk", 1)
        earlier.append(moving_up)
        moving_down = passed_along(moving_down, "blk", -1)
        later.append(moving_down)
    pieces = [earlier[1], earlier[0], coeffs, later[0], later[1]]
    window = jnp.concatenate(pieces, axis=0).reshape(5 * blocks_here, block_width, orbitals)
    owner = screen // blocks_here
    distance = (owner - position + loop_size) % loop_size
    distance = jnp.where(distance > loop_size // 2, distance - loop_size, distance)
    local_block = (distance + 2) * blocks_here + screen % blocks_here
    slot_index = jnp.arange(slot_count, dtype=jnp.int32)
    keep_slot = slot_index[None, :] < counts[:, None]
    picked = jnp.where(
        keep_slot[:, :, None, None], window[local_block], jnp.zeros((), jnp.bfloat16)
    )
    picked = picked.reshape(blocks_here, slot_count * block_width, orbitals)
    fit_blocks = fitting.reshape(blocks_here, block_width, aux_here, slot_count * block_width)
    half = jnp.einsum(
        "mupl,mli->mupi", fit_blocks, picked, preferred_element_type=jnp.float32
    ).astype(jnp.bfloat16)
    flat = half.reshape(blocks_here * block_width, aux_here * orbitals)
    total_aux = aux_here * lax.axis_size("aux")
    gram = lax.dot_general(flat, flat, (((1,), (1,)), ((), ())), preferred_element_type=jnp.float32)
    gram = gram / jnp.sqrt(jnp.float32(total_aux * orbitals))
    tiles = gram.reshape(blocks_here, block_width, blocks_here, block_width).transpose(0, 2, 1, 3)
    tiles = tiles.reshape(blocks_here * blocks_here, block_width * block_width)
    ordered = tiles[tile_order[0]]
    share = ordered.shape[0] // lax.axis_size("aux")
    summed = lax.psum(ordered, "aux")
    return lax.dynamic_slice_in_dim(summed, lax.axis_index("aux") * share, share, 0)


def solution(mesh):
    placed = (P("blk", None), P("blk", "aux", None), P("blk", None), P("blk"), P("blk", None))
    return jax.shard_map(
        per_device, mesh=mesh, in_specs=placed, out_specs=P(("blk", "aux"), None), check_vma=False
    )
```

profile of v0, /device:TPU:1, one launch (start us, length us, event | category | flops | bytes accessed | tf_op | source)
XLA Modules:
  0.0 137.2 jit_solution(14247176783398623179)
XLA Ops:
  6.5 3.7 %collective-permute-start = (bf16[256,512]{1,0:T(8,128)(2,1)}, bf16[256,512]{1,0:T(8,128)(2,1)S(1)}, u32[]{:S(2)}, u32[]{:S(2)}) collective-permute-start(bf16[256,512]{1,0:T(8,128)(2,1)} %param.5), channel_id=1, source_target_pairs={{0,4},{4,8},{8,12},{12,16},{16,20},{20,24},{24,28},{28,32},{32,36}... | collective-permute-start | bytes 786440 | tf_op jit(solution)/shard_map/ppermute | solution.py:9
  10.3 7.5 %collective-permute-start.2 = (bf16[256,512]{1,0:T(8,128)(2,1)}, bf16[256,512]{1,0:T(8,128)(2,1)S(1)}, u32[]{:S(2)}, u32[]{:S(2)}) collective-permute-start(bf16[256,512]{1,0:T(8,128)(2,1)} %param.5), channel_id=1, source_target_pairs={{0,252},{4,0},{8,4},{12,8},{16,12},{20,16},{24,20},{28,24},{32,28}... | collective-permute-start | bytes 786440 | tf_op jit(solution)/shard_map/ppermute | solution.py:9
  17.8 0.7 iota_compare_fusion
  18.5 0.7 compare_select_fusion
  19.2 4.8 %collective-permute-done = bf16[256,512]{1,0:T(8,128)(2,1)S(1)} collective-permute-done((bf16[256,512]{1,0:T(8,128)(2,1)}, bf16[256,512]{1,0:T(8,128)(2,1)S(1)}, u32[]{:S(2)}, u32[]{:S(2)}) %collective-permute-start) | collective-permute-done | bytes 262176 | tf_op jit(solution)/shard_map/ppermute | solution.py:9
  24.0 0.8 collective-permute-start.1
  24.8 0.7 fusion.8
  25.4 0.1 reshape.74
  25.5 0.1 broadcast_in_dim.23
  25.6 0.1 broadcast_in_dim.24
  25.7 7.6 %collective-permute-start.3 = (bf16[256,512]{1,0:T(8,128)(2,1)S(1)}, bf16[256,512]{1,0:T(8,128)(2,1)S(1)}, u32[]{:S(2)}, u32[]{:S(2)}) collective-permute-start(bf16[256,512]{1,0:T(8,128)(2,1)S(1)} %collective-permute-done.2), channel_id=1, source_target_pairs={{0,252},{4,0},{8,4},{12,8},{16,12},{20,16},{24,20},{28,24},{32,28}... | collective-permute-start | bytes 786440 | tf_op jit(solution)/shard_map/ppermute | solution.py:9
  33.3 4.1 %collective-permute-done.1 = bf16[256,512]{1,0:T(8,128)(2,1)S(1)} collective-permute-done((bf16[256,512]{1,0:T(8,128)(2,1)S(1)}, bf16[256,512]{1,0:T(8,128)(2,1)S(1)}, u32[]{:S(2)}, u32[]{:S(2)}) %collective-permute-start.1) | collective-permute-done | bytes 262176 | tf_op jit(solution)/shard_map/ppermute | solution.py:9
  37.4 1.0 constant_dynamic-update-slice_fusion.2
  38.4 0.6 gather_fusion
  39.1 0.2 bitcast_select_fusion
  39.3 11.6 %convolution_convert_fusion = bf16[4,512,64,64]{1,3,2,0:T(8,128)(2,1)} fusion(bf16[4,64,64,256]{3,2,1,0:T(8,128)(2,1)} %bitcast.29, bf16[4,256,512]{2,1,0:T(8,128)(2,1)S(1)} %bitcast_select_fusion), kind=kOutput, calls=%fused_computation.2 | convolution fusion | flops 4303355904 | bytes 26214400 | tf_op jit(solution)/shard_map/mupl,mli->mupi/dot_general | solution.py:42
  50.9 18.4 %copy.8 = bf16[32,8,64,512]{3,1,2,0:T(8,128)(2,1)} copy(bf16[32,8,64,512]{3,2,1,0:T(8,128)(2,1)} %bitcast.24) | data formatting | bytes 33554432
  69.3 12.9 %convolution_multiply_fusion = f32[256,256]{1,0:T(8,128)S(1)} fusion(bf16[256,32768]{1,0:T(8,128)(2,1)} %bitcast.25), kind=kOutput, calls=%fused_computation.3 | convolution fusion | flops 4295032832 | bytes 17039360 | tf_op jit(solution)/shard_map/dot_general | solution.py:47
  82.2 0.2 reshape.70
  82.5 0.1 copy.6
  82.6 0.2 reshape.71
  82.7 1.3 gather_fusion.1
  84.1 44.7 %all-reduce.2.cloned.1.call-done = f32[16,4096]{1,0:T(8,128)} async-done(((f32[16,4096]{1,0:T(8,128)}), f32[16,4096]{1,0:T(8,128)}) %all-reduce.2.cloned.1.call-update) | async-done | bytes 262160 | tf_op jit(solution)/shard_map/psum | solution.py:53
  128.8 1.5 %constant_dynamic-slice_fusion = f32[4,4096]{1,0:T(4,128)} fusion(f32[16,4096]{1,0:T(8,128)} %all-reduce.2.cloned.1.call-done, s32[]{:T(128)S(6)} %select_n.47), kind=kLoop, calls=%fused_computation.34 | loop fusion | bytes 131076 | tf_op jit(solution)/shard_map/dynamic_slice | solution.py:54
  (10 shorter events, 0.1 us)
Async XLA Ops:
  6.5 122.2 %all-reduce.2.cloned.1.call-start = ((), (), s32[]{:S(2)}) async-start(), calls=%async_computation | async-start | bytes 524288 | tf_op jit(solution)/shard_map/psum | solution.py:53
  6.5 17.5 %collective-permute-start = (bf16[256,512]{1,0:T(8,128)(2,1)}, bf16[256,512]{1,0:T(8,128)(2,1)S(1)}, u32[]{:S(2)}, u32[]{:S(2)}) collective-permute-start(bf16[256,512]{1,0:T(8,128)(2,1)} %param.5), channel_id=1, source_target_pairs={{0,4},{4,8},{8,12},{12,16},{16,20},{20,24},{24,28},{28,32},{32,36}... | collective-permute-start | bytes 786440 | tf_op jit(solution)/shard_map/ppermute | solution.py:9
  10.3 15.4 %collective-permute-start.2 = (bf16[256,512]{1,0:T(8,128)(2,1)}, bf16[256,512]{1,0:T(8,128)(2,1)S(1)}, u32[]{:S(2)}, u32[]{:S(2)}) collective-permute-start(bf16[256,512]{1,0:T(8,128)(2,1)} %param.5), channel_id=1, source_target_pairs={{0,252},{4,0},{8,4},{12,8},{16,12},{20,16},{24,20},{28,24},{32,28}... | collective-permute-start | bytes 786440 | tf_op jit(solution)/shard_map/ppermute | solution.py:9
  24.0 13.3 %collective-permute-start.1 = (bf16[256,512]{1,0:T(8,128)(2,1)S(1)}, bf16[256,512]{1,0:T(8,128)(2,1)S(1)}, u32[]{:S(2)}, u32[]{:S(2)}) collective-permute-start(bf16[256,512]{1,0:T(8,128)(2,1)S(1)} %collective-permute-done), channel_id=1, source_target_pairs={{0,4},{4,8},{8,12},{12,16},{16,20},{20,24},{24,28},{28,32},{32,36}... | collective-permute-start | bytes 786440 | tf_op jit(solution)/shard_map/ppermute | solution.py:9
  25.7 12.7 %collective-permute-start.3 = (bf16[256,512]{1,0:T(8,128)(2,1)S(1)}, bf16[256,512]{1,0:T(8,128)(2,1)S(1)}, u32[]{:S(2)}, u32[]{:S(2)}) collective-permute-start(bf16[256,512]{1,0:T(8,128)(2,1)S(1)} %collective-permute-done.2), channel_id=1, source_target_pairs={{0,252},{4,0},{8,4},{12,8},{16,12},{20,16},{24,20},{28,24},{32,28}... | collective-permute-start | bytes 786440 | tf_op jit(solution)/shard_map/ppermute | solution.py:9
Sparse Core Ops, SparseCore 0:
  84.2 44.5 all-reduce.1
where the time goes:
time: 138 us; the launch traced here: 137 us
  waiting for transfers between devices  53.6 us (39%)
  matrix products  24.5 us (18%)
  local copies, waits for them, and re-layouts  23.7 us (17%)
  starting transfers between devices  19.6 us (14%)
  between operations  13.5 us (10%)
  other arithmetic  2.3 us (2%)
    psum x1, waiting for transfers between devices, per_device(): summed = lax.psum(ordered, 'aux')  44.7 us
    ppermute x4, starting transfers between devices, passed_along(): lax.ppermute(value, axis, [(i, (i + by) % length) for i in range(length)])  19.6 us
    unnamed x5, local copies, waits for them, and re-layouts  19.5 us
    dot_general x1, matrix products, per_device(): lax.dot_general(flat, flat, (((1,), (1,)), ((), ())), preferred_element_t...  12.9 us
    dot_general x1, matrix products, per_device(): jnp.einsum('mupl,mli->mupi', fit_blocks, picked, preferred_element_type=j...  11.6 us
    ppermute x4, waiting for transfers between devices, passed_along(): lax.ppermute(value, axis, [(i, (i + by) % length) for i in range(length)])  8.87 us
  transfers between devices with their start and end apart: 5, of which 3 were waited for; matrix products, arithmetic and copies ran while one was open for 2% of the time, Pallas kernels for 0%

commit v1 on v0

--- a/solution.py
+++ b/solution.py
@@ -50,7 +50,7 @@
     tiles = tiles.reshape(blocks_here * blocks_here, block_width * block_width)
     ordered = tiles[tile_order[0]]
     share = ordered.shape[0] // lax.axis_size("aux")
-    summed = lax.psum(ordered, "aux")
+    summed = jnp.sum(lax.all_gather(ordered, "aux"), axis=0)
     return lax.dynamic_slice_in_dim(summed, lax.axis_index("aux") * share, share, 0)
 
 

time: 138 us -> 120 us (0.87)
  waiting for transfers between devices: 53.6 us -> 35.4 us
    psum x1 -> x0, waiting for transfers between devices: 44.7 us -> none  [per_device(): summed = lax.psum(ordered, 'aux')]
    all_gather x0 -> x1, waiting for transfers between devices: none -> 26.5 us  [per_device(): summed = jnp.sum(lax.all_gather(ordered, 'aux'), axis=0)]
  transfers between devices with their start and end apart: 5 -> 5, of which waited for: 3 -> 3; matrix products, arithmetic and copies ran while one was open for 2% -> 3% of each run, Pallas kernels for 0% -> 0%
where the time goes in v1:
time: 120 us; the launch traced here: 119 us
  waiting for transfers between devices  35.4 us (30%)
  matrix products  24.5 us (20%)
  local copies, waits for them, and re-layouts  22.8 us (19%)
  starting transfers between devices  19.6 us (16%)
  between operations  13.5 us (11%)
  other arithmetic  3.61 us (3%)
    all_gather x1, waiting for transfers between devices, per_device(): summed = jnp.sum(lax.all_gather(ordered, 'aux'), axis=0)  26.5 us
    ppermute x4, starting transfers between devices, passed_along(): lax.ppermute(value, axis, [(i, (i + by) % length) for i in range(length)])  19.6 us
    unnamed x5, local copies, waits for them, and re-layouts  19.5 us
    dot_general x1, matrix products, per_device(): lax.dot_general(flat, flat, (((1,), (1,)), ((), ())), preferred_element_t...  12.9 us
    dot_general x1, matrix products, per_device(): jnp.einsum('mupl,mli->mupi', fit_blocks, picked, preferred_element_type=j...  11.6 us
    ppermute x4, waiting for transfers between devices, passed_along(): lax.ppermute(value, axis, [(i, (i + by) % length) for i in range(length)])  8.87 us
  transfers between devices with their start and end apart: 5, of which 3 were waited for; matrix products, arithmetic and copies ran while one was open for 3% of the time, Pallas kernels for 0%

profile of v1, /device:TPU:1, one launch (start us, length us, event | category | flops | bytes accessed | tf_op | source)
XLA Modules:
  0.0 119.4 jit_solution(2609976904088654832)
XLA Ops:
  6.5 3.7 %collective-permute-start = (bf16[256,512]{1,0:T(8,128)(2,1)}, bf16[256,512]{1,0:T(8,128)(2,1)S(1)}, u32[]{:S(2)}, u32[]{:S(2)}) collective-permute-start(bf16[256,512]{1,0:T(8,128)(2,1)} %param.5), channel_id=1, source_target_pairs={{0,4},{4,8},{8,12},{12,16},{16,20},{20,24},{24,28},{28,32},{32,36}... | collective-permute-start | bytes 786440 | tf_op jit(solution)/shard_map/ppermute | solution.py:9
  10.3 7.5 %collective-permute-start.2 = (bf16[256,512]{1,0:T(8,128)(2,1)}, bf16[256,512]{1,0:T(8,128)(2,1)S(1)}, u32[]{:S(2)}, u32[]{:S(2)}) collective-permute-start(bf16[256,512]{1,0:T(8,128)(2,1)} %param.5), channel_id=1, source_target_pairs={{0,252},{4,0},{8,4},{12,8},{16,12},{20,16},{24,20},{28,24},{32,28}... | collective-permute-start | bytes 786440 | tf_op jit(solution)/shard_map/ppermute | solution.py:9
  17.8 0.7 iota_compare_fusion
  18.5 0.7 compare_select_fusion
  19.2 4.8 %collective-permute-done = bf16[256,512]{1,0:T(8,128)(2,1)S(1)} collective-permute-done((bf16[256,512]{1,0:T(8,128)(2,1)}, bf16[256,512]{1,0:T(8,128)(2,1)S(1)}, u32[]{:S(2)}, u32[]{:S(2)}) %collective-permute-start) | collective-permute-done | bytes 262176 | tf_op jit(solution)/shard_map/ppermute | solution.py:9
  24.0 0.8 collective-permute-start.1
  24.8 0.7 fusion.8
  25.4 0.1 reshape.74
  25.5 0.1 broadcast_in_dim.23
  25.6 0.1 broadcast_in_dim.24
  25.7 7.6 %collective-permute-start.3 = (bf16[256,512]{1,0:T(8,128)(2,1)S(1)}, bf16[256,512]{1,0:T(8,128)(2,1)S(1)}, u32[]{:S(2)}, u32[]{:S(2)}) collective-permute-start(bf16[256,512]{1,0:T(8,128)(2,1)S(1)} %collective-permute-done.2), channel_id=1, source_target_pairs={{0,252},{4,0},{8,4},{12,8},{16,12},{20,16},{24,20},{28,24},{32,28}... | collective-permute-start | bytes 786440 | tf_op jit(solution)/shard_map/ppermute | solution.py:9
  33.3 4.1 %collective-permute-done.1 = bf16[256,512]{1,0:T(8,128)(2,1)S(1)} collective-permute-done((bf16[256,512]{1,0:T(8,128)(2,1)S(1)}, bf16[256,512]{1,0:T(8,128)(2,1)S(1)}, u32[]{:S(2)}, u32[]{:S(2)}) %collective-permute-start.1) | collective-permute-done | bytes 262176 | tf_op jit(solution)/shard_map/ppermute | solution.py:9
  37.4 1.0 constant_dynamic-update-slice_fusion.2
  38.4 0.6 gather_fusion
  39.1 0.2 bitcast_select_fusion
  39.3 11.6 %convolution_convert_fusion = bf16[4,512,64,64]{1,3,2,0:T(8,128)(2,1)} fusion(bf16[4,64,64,256]{3,2,1,0:T(8,128)(2,1)} %bitcast.31, bf16[4,256,512]{2,1,0:T(8,128)(2,1)S(1)} %bitcast_select_fusion), kind=kOutput, calls=%fused_computation.2 | convolution fusion | flops 4303355904 | bytes 26214400 | tf_op jit(solution)/shard_map/mupl,mli->mupi/dot_general | solution.py:42
  50.9 18.4 %copy.8 = bf16[32,8,64,512]{3,1,2,0:T(8,128)(2,1)} copy(bf16[32,8,64,512]{3,2,1,0:T(8,128)(2,1)} %bitcast.25) | data formatting | bytes 33554432
  69.3 12.9 %convolution_multiply_fusion = f32[256,256]{1,0:T(8,128)S(1)} fusion(bf16[256,32768]{1,0:T(8,128)(2,1)} %bitcast.26), kind=kOutput, calls=%fused_computation.3 | convolution fusion | flops 4295032832 | bytes 17039360 | tf_op jit(solution)/shard_map/dot_general | solution.py:47
  82.2 0.2 reshape.70
  82.6 0.2 reshape.71
  82.7 1.3 %gather_fusion.1 = f32[16,4096]{1,0:T(8,128)} fusion(f32[16,4096]{1,0:T(8,128)S(1)} %reshape.71, s32[1024]{0:T(1024)S(1)} %pad_clamp_fusion), kind=kCustom, calls=%fused_computation.1 | custom fusion | bytes 524352 | tf_op jit(solution)/shard_map/gather | solution.py:51
  84.1 26.5 %all-gather.3.cloned.1.call-done = f32[64,4096]{1,0:T(8,128)} async-done(((f32[16,4096]{1,0:T(8,128)}), f32[64,4096]{1,0:T(8,128)}) %all-gather.3.cloned.1.call-update) | async-done | bytes 1048592 | tf_op jit(solution)/shard_map/all_gather | solution.py:53
  110.6 1.3 %reduce_sum.9 = f32[16,4096]{1,0:T(8,128)S(1)} reduce(f32[4,16,4096]{2,1,0:T(8,128)} %bitcast.30, f32[]{:T(128)} %constant.68.clone.1), dimensions={0}, to_apply=%region_0.1 | reduce | flops 196608 | bytes 1310724 | tf_op jit(solution)/shard_map/reduce_sum | solution.py:53
  111.9 0.7 constant_dynamic-slice_fusion
  (11 shorter events, 0.2 us)
Async XLA Ops:
  6.5 104.0 %all-gather.3.cloned.1.call-start = ((), (), s32[]{:S(2)}) async-start(), calls=%async_computation | async-start | bytes 1310720 | tf_op jit(solution)/shard_map/all_gather | solution.py:53
  6.5 17.5 %collective-permute-start = (bf16[256,512]{1,0:T(8,128)(2,1)}, bf16[256,512]{1,0:T(8,128)(2,1)S(1)}, u32[]{:S(2)}, u32[]{:S(2)}) collective-permute-start(bf16[256,512]{1,0:T(8,128)(2,1)} %param.5), channel_id=1, source_target_pairs={{0,4},{4,8},{8,12},{12,16},{16,20},{20,24},{24,28},{28,32},{32,36}... | collective-permute-start | bytes 786440 | tf_op jit(solution)/shard_map/ppermute | solution.py:9
  10.3 15.4 %collective-permute-start.2 = (bf16[256,512]{1,0:T(8,128)(2,1)}, bf16[256,512]{1,0:T(8,128)(2,1)S(1)}, u32[]{:S(2)}, u32[]{:S(2)}) collective-permute-start(bf16[256,512]{1,0:T(8,128)(2,1)} %param.5), channel_id=1, source_target_pairs={{0,252},{4,0},{8,4},{12,8},{16,12},{20,16},{24,20},{28,24},{32,28}... | collective-permute-start | bytes 786440 | tf_op jit(solution)/shard_map/ppermute | solution.py:9
  24.0 13.3 %collective-permute-start.1 = (bf16[256,512]{1,0:T(8,128)(2,1)S(1)}, bf16[256,512]{1,0:T(8,128)(2,1)S(1)}, u32[]{:S(2)}, u32[]{:S(2)}) collective-permute-start(bf16[256,512]{1,0:T(8,128)(2,1)S(1)} %collective-permute-done), channel_id=1, source_target_pairs={{0,4},{4,8},{8,12},{12,16},{16,20},{20,24},{24,28},{28,32},{32,36}... | collective-permute-start | bytes 786440 | tf_op jit(solution)/shard_map/ppermute | solution.py:9
  25.7 12.7 %collective-permute-start.3 = (bf16[256,512]{1,0:T(8,128)(2,1)S(1)}, bf16[256,512]{1,0:T(8,128)(2,1)S(1)}, u32[]{:S(2)}, u32[]{:S(2)}) collective-permute-start(bf16[256,512]{1,0:T(8,128)(2,1)S(1)} %collective-permute-done.2), channel_id=1, source_target_pairs={{0,252},{4,0},{8,4},{12,8},{16,12},{20,16},{24,20},{28,24},{32,28}... | collective-permute-start | bytes 786440 | tf_op jit(solution)/shard_map/ppermute | solution.py:9
Sparse Core Ops, SparseCore 0:
  84.2 26.3 all-gather.2
